TPU v7x, 256 devices: a whole 4x4x8 slice. The times are simulated.
256 devices in a mesh: band: 8 (over x, core), grid: 32 (over z, y).
Axes of the slice: x: 4, y: 4, z: 8, core: 2. Of those that a mesh axis runs over, the one named last changes fastest.
Arguments:
- coeffs: float32 [2, 8, 22016, 128], P(None, 'band', 'grid'), may hold values from -6 to 6
- stick_ids: int32 [22016], replicated, may hold values from -1 to 16383, as said below
- band_weights: float32 [8], P('band'), may hold values from 0.02 to 0.2
- aug_functions: float32 [128, 16, 256], replicated, may hold values from -0.1875 to 0.1875
- atom_offsets: int32 [64, 3], replicated, may hold values from 0 to 255, as said below
- intersection_list: int32 [32, 7], P('grid'), may hold values from 0 to 63, as said below
- atom_slots: int32 [128], replicated, may hold values from -1 to 63, as said below
Outputs:
- density: float32 [256, 256, 256], P('grid', 'band')
- atom_totals: float32 [128, 128, 128], P('grid')
Inputs may be any that keep to these rules, and one draw needn't show every extreme that they name: `stick_ids`: every column of the 128 x 128 wave-vector columns stands in exactly one slot; empty slots hold -1; some index of grid has all its 688 slots filled. `atom_slots`: every atom stands in exactly one slot; empty slots hold -1; some index of grid has all its 4 slots filled. `atom_offsets`: columns are x0, y0, z0; atom a has z0 in a * 4 .. (a + 1) * 4 - 1. `intersection_list`: row d names 7 distinct atoms, among them every atom whose box has a layer on the planes of index d of grid.
All inputs are finite; a program needn't handle non-finite values.
Results may differ from a plain program's by a relative error of at most 0.0003.
Values sent between devices are 32-bit elements; how exact they have to be, the bound alone decides.
A program may use at most 192 MiB of HBM per device.

v0:
```python
import jax
import jax.numpy as jnp
from jax import lax
from jax.sharding import PartitionSpec as P

GRID = 256
KG = 128
BOX = 16
NFUNC = 128
HIGH = lax.Precision.HIGHEST


def dft_tables(amount, length):
    frequency = jnp.arange(amount, dtype=jnp.int32) - amount // 2
    points = jnp.arange(length, dtype=jnp.int32)
    phases = frequency[:, None] * points[None, :] % length
    angles = phases.astype(jnp.float32) * (2.0 * jnp.pi / length)
    factor = amount ** (-0.5)
    return (jnp.cos(angles) * factor, jnp.sin(angles) * factor)


def complex_apply(form, real_part, imag_part, cosine, sine):
    real_out = jnp.einsum(form, real_part, cosine, precision=HIGH) - jnp.einsum(
        form, imag_part, sine, precision=HIGH
    )
    imag_out = jnp.einsum(form, real_part, sine, precision=HIGH) + jnp.einsum(
        form, imag_part, cosine, precision=HIGH
    )
    return (real_out, imag_out)


def column_slots(stick_ids):
    total = KG * KG
    target = jnp.where(stick_ids >= 0, stick_ids, total)
    filled = (
        jnp.zeros((total + 1,), jnp.int32)
        .at[target]
        .set(jnp.arange(stick_ids.shape[0], dtype=jnp.int32))
    )
    return filled[:total]


def layer_pick(first, lowest, layers, planes):
    planes_here = first + jnp.arange(planes, dtype=jnp.int32)
    depth = (planes_here - lowest) % GRID
    return (depth[:, None] == layers[None, :]).astype(jnp.float32)


def wrap_pad(field):
    field = jnp.concatenate([field, field[..., :BOX, :]], axis=-2)
    return jnp.concatenate([field, field[..., :BOX]], axis=-1)


def fold_pad(padded):
    rows = padded[:, :GRID, :] + jnp.pad(padded[:, GRID:, :], ((0, 0), (0, GRID - BOX), (0, 0)))
    return rows[:, :, :GRID] + jnp.pad(rows[:, :, GRID:], ((0, 0), (0, 0), (0, GRID - BOX)))


def on_device(
    coeffs, stick_ids, band_weights, aug_functions, atom_offsets, intersection_list, atom_slots
):
    planes = GRID // lax.axis_size("grid")
    first_plane = lax.axis_index("grid") * planes
    listed = intersection_list[0]
    listed_offsets = atom_offsets[listed]
    listed_count = listed.shape[0]
    own_rows = atom_slots.shape[0] // lax.axis_size("grid")
    every_layer = jnp.arange(BOX, dtype=jnp.int32)
    cosine, sine = dft_tables(KG, GRID)
    slot_map = column_slots(stick_ids)
    z_real, z_imag = complex_apply("bsg,gn->bns", coeffs[0], coeffs[1], cosine, sine)
    sticks = jnp.stack([z_real, z_imag])

    def project_atom(padded_wave, offsets):
        bands_here = padded_wave.shape[1]
        pick = layer_pick(first_plane, offsets[2], every_layer, planes)
        chosen = jnp.einsum("pk,ikc->ipc", pick, aug_functions, precision=HIGH)
        window = lax.dynamic_slice(
            padded_wave, (0, 0, 0, offsets[0], offsets[1]), (2, bands_here, planes, BOX, BOX)
        )
        window = window.reshape(2, bands_here, planes, BOX * BOX)
        return jnp.einsum("ipc,xbpc->bxi", chosen, window, precision=HIGH)

    received = lax.all_to_all(sticks, "grid", split_axis=2, concat_axis=3, tiled=True)
    bands_here = received.shape[1]
    spectra = received[:, :, :, slot_map].reshape(2, bands_here, planes, KG, KG)
    y_real, y_imag = complex_apply("bpxy,yn->bpxn", spectra[0], spectra[1], cosine, sine)
    x_real, x_imag = complex_apply("bpxn,xm->bpmn", y_real, y_imag, cosine, sine)
    band_density = x_real * x_real + x_imag * x_imag
    padded_wave = wrap_pad(jnp.stack([x_real, x_imag]))
    found = jax.vmap(lambda offsets: project_atom(padded_wave, offsets), out_axes=1)(listed_offsets)
    density = jnp.einsum("b,bpxy->pxy", band_weights, band_density, precision=HIGH)
    flat_found = jnp.transpose(found, (1, 0, 2, 3)).reshape(listed_count, -1)
    pick = (atom_slots[:, None] == listed[None, :]).astype(jnp.float32)
    owned = lax.psum_scatter(
        jnp.dot(pick, flat_found, precision=HIGH), "grid", scatter_dimension=0, tiled=True
    )
    owned = owned.reshape(own_rows, band_weights.shape[0], 2, NFUNC)
    partial_matrices = jnp.einsum("b,sbxi,sbxj->sij", band_weights, owned, owned, precision=HIGH)
    atom_totals = lax.psum(partial_matrices, "band")
    slot_pick = (listed[:, None] == atom_slots[None, :]).astype(jnp.float32)
    thickness = BOX // lax.axis_size("band")
    band_layers = lax.axis_index("band") * thickness + jnp.arange(thickness, dtype=jnp.int32)
    layers_here = lax.dynamic_slice_in_dim(
        aug_functions, lax.axis_index("band") * thickness, thickness, 1
    )
    layers_here = layers_here.reshape(NFUNC, thickness * BOX * BOX)
    halfway = jnp.einsum("sij,jc->sic", atom_totals, layers_here, precision=HIGH)
    box_part = jnp.sum(halfway * layers_here[None], axis=1)
    every_box = lax.all_gather(box_part, "grid", axis=0, tiled=True)
    mine = jnp.dot(slot_pick, every_box, precision=HIGH).reshape(listed_count, thickness, BOX * BOX)

    def box_piece(offsets, box_rows):
        pick = layer_pick(first_plane, offsets[2], band_layers, planes)
        return jnp.dot(pick, box_rows, precision=HIGH).reshape(planes, BOX, BOX)

    pieces = jax.vmap(box_piece)(listed_offsets, mine)

    def place(index, acc):
        corner = (0, listed_offsets[index, 0], listed_offsets[index, 1])
        current = lax.dynamic_slice(acc, corner, (planes, BOX, BOX))
        return lax.dynamic_update_slice(acc, current + pieces[index], corner)

    padded = lax.fori_loop(
        0, listed_count, place, jnp.zeros((planes, GRID + BOX, GRID + BOX), jnp.float32)
    )
    total = density + fold_pad(padded)
    result = lax.psum_scatter(total, "band", scatter_dimension=1, tiled=True)
    return (result, atom_totals)


def solution(mesh):
    placed = (P(None, "band", "grid", None), P(), P("band"), P(), P(), P("grid", None), P())
    return jax.shard_map(
        on_device,
        mesh=mesh,
        in_specs=placed,
        out_specs=(P("grid", "band", None), P("grid", None, None)),
        check_vma=False,
    )
```

profile of v0, /device:TPU:8, one launch (start us, length us, event | category | flops | bytes accessed | tf_op | source)
XLA Modules:
  0.0 786.7 jit_solution(15550919658142856036)
XLA Ops:
  7.2 2.4 fusion.16
  15.4 3.0 copy.39
  18.4 11.9 %all-to-all-start = ((f32[2,1,256,688]{3,1,0,2:T(1,128)}), f32[2,1,256,688]{3,1,0,2:T(1,128)}, u32[]{:S(2)}, u32[]{:S(2)}) async-start(f32[2,1,256,688]{3,1,0,2:T(1,128)} %copy.39), calls=%async_computation | async-start | bytes 3145728 | tf_op jit(solution)/shard_map/all_to_all | solution.py:84
  31.3 81.4 %scatter_custom_fusion = s32[16385]{0:T(1024)S(1)} fusion(s32[22016]{0:T(1024)S(1)} %compare_select_fusion, s32[22016]{0:T(1024)S(1)} %iota.50, s32[]{:T(128)} %constant.80.clone.1), kind=kCustom, calls=%fused_computation.75 | custom fusion | bytes 65544 | tf_op jit(solution)/shard_map/scatter | solution.py:38
  113.0 5.2 convolution_bitcast_fusion
  118.2 2.7 copy.87
  120.9 21.8 %copy.67 = f32[2,1,8,32,688]{2,0,4,3,1:T(2,128)} copy(f32[2,1,8,32,688]{4,2,3,0,1:T(8,128)} %bitcast.131) | data formatting | bytes 2818048 | tf_op jit(solution)/shard_map/all_to_all | solution.py:84
  142.7 118.9 %gather_fusion = f32[16384,2,8]{2,1,0:T(2,128)} fusion(f32[2,8,22016]{1,0,2:T(2,128)} %bitcast.129, s32[16384]{0:T(1024)S(1)} %fusion.42), kind=kCustom, calls=%fused_computation | custom fusion | bytes 2162688 | tf_op jit(solution)/shard_map/gather | solution.py:86
  261.6 19.3 %fusion.133 = (f32[1,8,16384]{1,0,2:T(1,128)}, f32[1,8,16384]{1,0,2:T(1,128)}) fusion(f32[2,8,16384]{1,0,2:T(2,128)} %bitcast.130), kind=kLoop, calls=%fused_computation.178 | loop fusion | bytes 2097152 | tf_op jit(solution)/shard_map/slice | solution.py:87
  280.9 5.1 copy.68
  286.1 2.5 fusion.34
  288.6 2.4 fusion.27
  291.0 5.3 copy.70
  296.3 2.7 convolution_subtract_fusion.1
  307.5 2.3 convolution_add_fusion
  311.2 3.0 fusion.2
  314.1 75.1 %copy.53 = f32[2,1,8,272,272]{2,0,1,4,3:T(2,128)} copy(f32[2,1,8,272,272]{4,3,2,1,0:T(8,128)} %fusion.2) | data formatting | bytes 9469952 | tf_op jit(solution)/shard_map/concatenate | solution.py:51
  389.2 5.3 gather_fusion.2
  394.5 2.6 copy.54
  397.2 9.8 %fusion.11 = f32[1,7,2,128]{3,2,1,0:T(2,128)S(1)} fusion(f32[7,2,8,256]{3,1,2,0:T(2,128)S(1)} %copy.54, f32[7,128,8,256]{3,2,1,0:T(8,128)} %convolution_bitcast_fusion), kind=kOutput, calls=%fused_computation.34 | convolution fusion | flops 44040192 | bytes 7461888 | tf_op jit(solution)/shard_map/vmap(ipc,xbpc->bxi)/dot_general | solution.py:82
  409.9 141.7 %all-reduce.8.cloned.1.call-done = f32[128,256]{1,0:T(8,128)} async-done(((f32[128,256]{1,0:T(8,128)}), f32[128,256]{1,0:T(8,128)}) %all-reduce.8.cloned.1.call-update) | async-done | bytes 131088
  554.2 64.0 %all-reduce.6.cloned.1.call-done = f32[4,128,128]{2,1,0:T(8,128)} async-done(((f32[4,128,128]{2,1,0:T(8,128)}), f32[4,128,128]{2,1,0:T(8,128)}) %all-reduce.6.cloned.1.call-update) | async-done | bytes 262160 | tf_op jit(solution)/shard_map/psum | solution.py:100
  620.1 49.4 %all-gather = f32[32,4,512]{2,1,0:T(4,128)S(1)} all-gather(f32[1,4,512]{2,1,0:T(4,128)S(1)} %bitcast.135), channel_id=1, replica_groups=mesh['band'=8,'grid'=32] {'grid'}, dimensions={0}, use_global_device_ids=true | all-gather | bytes 270336 | tf_op jit(solution)/shard_map/all_gather | solution.py:110
  672.2 67.8 %while.13 = (s32[]{:T(128)}, f32[8,272,272]{2,1,0:T(8,128)}, s32[7,3]{0,1:T(4,128)S(1)}, f32[7,8,16,16]{3,2,1,0:T(8,128)S(1)}, s32[]{:T(128)}, /*index=5*/s32[]{:T(128)}, s32[]{:T(128)}) while((s32[]{:T(128)}, f32[8,272,272]{2,1,0:T(8,128)}, s32[7,3]{0,1:T(4,128)S(1)}, f32[7,8,16,16]{3,2,1,0:T(8,128)S(1)}, s32[]{:T(128)}, ...), condition=%wide.region_5.6_spmd, body=%wide.region_4.5_spmd.sunk | while | flops 2056 | bytes 41141 | solution.py:124
  677.7 4.3 dynamic_update_slice.8
  687.4 4.3 dynamic_update_slice.8
  697.1 4.2 dynamic_update_slice.8
  706.7 4.3 dynamic_update_slice.8
  716.4 4.3 dynamic_update_slice.8
  726.1 4.3 dynamic_update_slice.8
  735.8 4.3 dynamic_update_slice.8
  745.9 33.3 %reduce-scatter.2.cloned.1.call-done = f32[8,32,256]{2,1,0:T(8,128)} async-done(((f32[8,256,256]{2,1,0:T(8,128)}), f32[8,32,256]{2,1,0:T(8,128)}) %reduce-scatter.2.cloned.1.call-update) | async-done | bytes 262160 | tf_op jit(solution)/shard_map/reduce_scatter | solution.py:128
  (90 shorter events, 43.5 us)
Async XLA Ops:
  7.2 105.8 %copy-start = (f32[128,16,256]{2,1,0:T(8,128)S(1)}, f32[128,16,256]{2,1,0:T(8,128)}, u32[]{:S(2)}) copy-start(f32[128,16,256]{2,1,0:T(8,128)} %param.12) | copy-start | bytes 6291460
  7.2 6.8 copy-start.6
  15.4 14.9 %copy-start.11 = (s32[64,3]{0,1:T(4,128)S(1)}, s32[64,3]{0,1:T(4,128)}, u32[]{:S(2)}) copy-start(s32[64,3]{0,1:T(4,128)} %param.13) | copy-start | bytes 2308
  15.4 15.0 %copy-start.9 = (s32[1,7]{1,0:T(1,128)S(1)}, s32[1,7]{1,0:T(1,128)}, u32[]{:S(2)}) copy-start(s32[1,7]{1,0:T(1,128)} %param.14) | copy-start | bytes 88
  18.4 12.8 %copy-start.8 = (s32[22016]{0:T(1024)S(1)}, s32[22016]{0:T(1024)}, u32[]{:S(2)}) copy-start(s32[22016]{0:T(1024)} %param.10) | copy-start | bytes 264196
  18.4 99.8 %all-to-all-start = ((f32[2,1,256,688]{3,1,0,2:T(1,128)}), f32[2,1,256,688]{3,1,0,2:T(1,128)}, u32[]{:S(2)}, u32[]{:S(2)}) async-start(f32[2,1,256,688]{3,1,0,2:T(1,128)} %copy.39), calls=%async_computation | async-start | bytes 3145728 | tf_op jit(solution)/shard_map/all_to_all | solution.py:84
  30.3 521.3 %all-reduce.8.cloned.1.call-start = ((), (), s32[]{:S(2)}) async-start(), calls=%async_computation.4 | async-start | bytes 262144
  299.1 4.6 copy-start.5
  307.5 2.4 copy-start.1
  309.8 1.3 copy-start.3
  397.2 9.8 %copy-start.10 = (s32[128]{0:T(128)S(1)}, s32[128]{0:T(128)}, u32[]{:S(2)}) copy-start(s32[128]{0:T(128)} %param.15) | copy-start | bytes 1540
  397.2 11.4 %copy-start.12 = (u32[256]{0:T(256)S(1)}, u32[256]{0:T(256)}, u32[]{:S(2)}) copy-start(u32[256]{0:T(256)} %constant.145) | copy-start | bytes 3076
  407.9 210.2 %all-reduce.6.cloned.1.call-start = ((), (), s32[]{:S(2)}) async-start(), calls=%async_computation.2 | async-start | bytes 524288 | tf_op jit(solution)/shard_map/psum | solution.py:100
  553.6 225.6 %reduce-scatter.2.cloned.1.call-start = ((), (), s32[]{:S(2)}) async-start(), calls=%async_computation.3 | async-start | bytes 2359296 | tf_op jit(solution)/shard_map/reduce_scatter | solution.py:128
  741.0 2.5 copy-start.2
  741.0 3.2 copy-start.4
  744.2 35.1 %copy-start.7 = (f32[4,128,128]{2,1,0:T(8,128)S(1)}, f32[4,128,128]{2,1,0:T(8,128)}, u32[]{:S(2)}) copy-start(f32[4,128,128]{2,1,0:T(8,128)} %all-reduce.6.cloned.1.call-done) | copy-start | bytes 786436
Sparse Core Ops, SparseCore 0:
  408.0 143.4 all-reduce.7
  554.5 63.6 all-reduce.5
  746.1 33.1 reduce-scatter.1
where the time goes:
time: 800 us; the launch traced here: 787 us
  local copies, waits for them, and re-layouts  383 us (48%)
  waiting for transfers between devices  239 us (30%)
  blocking collectives  49.4 us (6%)
  matrix products  46 us (6%)
  loops' own time  26.6 us (3%)
  between operations  15.7 us (2%)
  other arithmetic  14.8 us (2%)
  starting transfers between devices  12 us (2%)
    unnamed x4, waiting for transfers between devices  142 us
    gather x1, local copies, waits for them, and re-layouts, on_device(): spectra = received[:, :, :, slot_map].reshape(2, bands_here, planes, KG, KG)  119 us
    scatter x1, local copies, waits for them, and re-layouts, column_slots(): filled = jnp.zeros((total + 1,), jnp.int32).at[target].set(jnp.arange(sti...  81.4 us
    concatenate x1, local copies, waits for them, and re-layouts, wrap_pad(): return jnp.concatenate([field, field[..., :BOX]], axis=-1)  75.1 us
    psum x1, waiting for transfers between devices, on_device(): atom_totals = lax.psum(partial_matrices, 'band')  64 us
    all_gather x1, blocking collectives, on_device(): every_box = lax.all_gather(box_part, 'grid', axis=0, tiled=True)  49.4 us
    reduce_scatter x1, waiting for transfers between devices, on_device(): result = lax.psum_scatter(total, 'band', scatter_dimension=1, tiled=True)  33.3 us
    dynamic_update_slice x7, local copies, waits for them, and re-layouts, place(): return lax.dynamic_update_slice(acc, current + pieces[index], corner)  29.9 us
  transfers between devices with their start and end apart: 4, of which 3 were waited for; matrix products, arithmetic and copies ran while one was open for 11% of the time, Pallas kernels for 0%

commit v1 on v0

--- a/solution.py
+++ b/solution.py
@@ -8,6 +8,15 @@
 BOX = 16
 NFUNC = 128
 HIGH = lax.Precision.HIGHEST
+_advance_column = lambda pos_dim, s0: jnp.concatenate(
+    jax.lax.all_to_all(
+        jnp.stack([s0 for _ in range(jax.lax.axis_size("grid"))], 0),
+        "grid",
+        split_axis=0,
+        concat_axis=0,
+    ),
+    pos_dim,
+)
 
 
 def dft_tables(amount, length):
@@ -107,7 +116,7 @@
     layers_here = layers_here.reshape(NFUNC, thickness * BOX * BOX)
     halfway = jnp.einsum("sij,jc->sic", atom_totals, layers_here, precision=HIGH)
     box_part = jnp.sum(halfway * layers_here[None], axis=1)
-    every_box = lax.all_gather(box_part, "grid", axis=0, tiled=True)
+    every_box = _advance_column(0, box_part)
     mine = jnp.dot(slot_pick, every_box, precision=HIGH).reshape(listed_count, thickness, BOX * BOX)
 
     def box_piece(offsets, box_rows):

time: 800 us -> 773 us (0.966)
  blocking collectives: 49.4 us -> 0 us
  starting transfers between devices: 12 us -> 22.2 us
  waiting for transfers between devices: 239 us -> 249 us
    all_gather x1 -> x0, blocking collectives: 49.4 us -> none  [on_device(): every_box = lax.all_gather(box_part, 'grid', axis=0, tiled=True)]
    all_to_all x0 -> x1, starting transfers between devices: none -> 10.2 us  [jax.lax.all_to_all(jnp.stack([s0 for _ in range(jax.lax.axis_size('grid')...]
    all_to_all x0 -> x1, waiting for transfers between devices: none -> 9.58 us  [jax.lax.all_to_all(jnp.stack([s0 for _ in range(jax.lax.axis_size('grid')...]
  transfers between devices with their start and end apart: 4 -> 5, of which waited for: 3 -> 4; matrix products, arithmetic and copies ran while one was open for 11% -> 12% of each run, Pallas kernels for 0% -> 0%
where the time goes in v1:
time: 773 us; the launch traced here: 760 us
  local copies, waits for them, and re-layouts  384 us (50%)
  waiting for transfers between devices  249 us (32%)
  matrix products  46.1 us (6%)
  loops' own time  28.1 us (4%)
  starting transfers between devices  22.2 us (3%)
  between operations  15.7 us (2%)
  other arithmetic  14.8 us (2%)
    unnamed x4, waiting for transfers between devices  142 us
    gather x1, local copies, waits for them, and re-layouts, on_device(): spectra = received[:, :, :, slot_map].reshape(2, bands_here, planes, KG, KG)  119 us
    scatter x1, local copies, waits for them, and re-layouts, column_slots(): filled = jnp.zeros((total + 1,), jnp.int32).at[target].set(jnp.arange(sti...  81.4 us
    concatenate x1, local copies, waits for them, and re-layouts, wrap_pad(): return jnp.concatenate([field, field[..., :BOX]], axis=-1)  74.9 us
    psum x1, waiting for transfers between devices, on_device(): atom_totals = lax.psum(partial_matrices, 'band')  64.1 us
    reduce_scatter x1, waiting for transfers between devices, on_device(): result = lax.psum_scatter(total, 'band', scatter_dimension=1, tiled=True)  33.1 us
    dynamic_update_slice x7, local copies, waits for them, and re-layouts, place(): return lax.dynamic_update_slice(acc, current + pieces[index], corner)  29.9 us
    another operation x1, loops' own time, on_device(): lax.fori_loop(0, listed_count, place, jnp.zeros((planes, GRID + BOX, GRID...  28.1 us
  transfers between devices with their start and end apart: 5, of which 4 were waited for; matrix products, arithmetic and copies ran while one was open for 12% of the time, Pallas kernels for 0%

profile of v1, /device:TPU:8, one launch (start us, length us, event | category | flops | bytes accessed | tf_op | source)
XLA Modules:
  0.0 759.6 jit_solution(1231596197057272579)
XLA Ops:
  7.2 2.4 fusion.16
  15.4 3.0 copy.61
  18.4 11.9 %all-to-all-start = ((f32[2,1,256,688]{3,1,0,2:T(1,128)}), f32[2,1,256,688]{3,1,0,2:T(1,128)}, u32[]{:S(2)}, u32[]{:S(2)}) async-start(f32[2,1,256,688]{3,1,0,2:T(1,128)} %copy.61), calls=%async_computation | async-start | bytes 3145728 | tf_op jit(solution)/shard_map/all_to_all | solution.py:93
  31.3 81.4 %scatter_custom_fusion = s32[16385]{0:T(1024)S(1)} fusion(s32[22016]{0:T(1024)S(1)} %compare_select_fusion, s32[22016]{0:T(1024)S(1)} %iota.50, s32[]{:T(128)} %constant.80.clone.1), kind=kCustom, calls=%fused_computation.75 | custom fusion | bytes 65544 | tf_op jit(solution)/shard_map/scatter | solution.py:47
  113.0 5.2 convolution_bitcast_fusion
  118.1 2.7 copy.113
  120.8 21.8 %copy.91 = f32[2,1,8,32,688]{2,0,4,3,1:T(2,128)} copy(f32[2,1,8,32,688]{4,2,3,0,1:T(8,128)} %bitcast.134) | data formatting | bytes 2818048 | tf_op jit(solution)/shard_map/all_to_all | solution.py:93
  142.7 118.8 %gather_fusion = f32[16384,2,8]{2,1,0:T(2,128)} fusion(f32[2,8,22016]{1,0,2:T(2,128)} %bitcast.132, s32[16384]{0:T(1024)S(1)} %fusion.42), kind=kCustom, calls=%fused_computation | custom fusion | bytes 2162688 | tf_op jit(solution)/shard_map/gather | solution.py:95
  261.5 19.3 %fusion.135 = (f32[1,8,16384]{1,0,2:T(1,128)}, f32[1,8,16384]{1,0,2:T(1,128)}) fusion(f32[2,8,16384]{1,0,2:T(2,128)} %bitcast.133), kind=kLoop, calls=%fused_computation.180 | loop fusion | bytes 2097152 | tf_op jit(solution)/shard_map/slice | solution.py:96
  280.8 5.1 copy.92
  285.9 2.5 fusion.34
  288.4 2.4 fusion.27
  290.9 5.3 copy.94
  296.2 2.7 convolution_subtract_fusion.1
  311.0 3.0 fusion.2
  314.0 74.9 %copy.75 = f32[2,1,8,272,272]{2,0,1,4,3:T(2,128)} copy(f32[2,1,8,272,272]{4,3,2,1,0:T(8,128)} %fusion.2) | data formatting | bytes 9469952 | tf_op jit(solution)/shard_map/concatenate | solution.py:60
  388.9 5.3 gather_fusion.2
  394.2 2.6 copy.76
  396.8 9.8 %fusion.11 = f32[1,7,2,128]{3,2,1,0:T(2,128)S(1)} fusion(f32[7,2,8,256]{3,1,2,0:T(2,128)S(1)} %copy.76, f32[7,128,8,256]{3,2,1,0:T(8,128)} %convolution_bitcast_fusion), kind=kOutput, calls=%fused_computation.34 | convolution fusion | flops 44040192 | bytes 7461888 | tf_op jit(solution)/shard_map/vmap(ipc,xbpc->bxi)/dot_general | solution.py:91
  409.5 141.7 %all-reduce.8.cloned.1.call-done = f32[128,256]{1,0:T(8,128)} async-done(((f32[128,256]{1,0:T(8,128)}), f32[128,256]{1,0:T(8,128)}) %all-reduce.8.cloned.1.call-update) | async-done | bytes 131088
  553.7 64.1 %all-reduce.6.cloned.1.call-done = f32[4,128,128]{2,1,0:T(8,128)} async-done(((f32[4,128,128]{2,1,0:T(8,128)}), f32[4,128,128]{2,1,0:T(8,128)}) %all-reduce.6.cloned.1.call-update) | async-done | bytes 262160 | tf_op jit(solution)/shard_map/psum | solution.py:109
  620.5 10.2 %all-to-all-start.1 = ((f32[32,4,512]{2,1,0:T(4,128)}), f32[32,4,512]{2,1,0:T(4,128)S(1)}, u32[]{:S(2)}, u32[]{:S(2)}) async-start(f32[32,4,512]{2,1,0:T(4,128)} %stack.20), calls=%async_computation.1 | async-start | bytes 524288 | tf_op jit(solution)/shard_map/all_to_all | solution.py:12
  630.8 9.6 %all-to-all-done.1 = f32[32,4,512]{2,1,0:T(4,128)S(1)} async-done(((f32[32,4,512]{2,1,0:T(4,128)}), f32[32,4,512]{2,1,0:T(4,128)S(1)}, u32[]{:S(2)}, u32[]{:S(2)}) %all-to-all-start.1) | async-done | bytes 262176 | tf_op jit(solution)/shard_map/all_to_all | solution.py:12
  643.3 69.9 %while.13 = (s32[]{:T(128)}, f32[8,272,272]{2,1,0:T(8,128)}, s32[7,3]{0,1:T(4,128)S(1)}, f32[7,8,16,16]{3,2,1,0:T(8,128)S(1)}, s32[]{:T(128)}, /*index=5*/s32[]{:T(128)}, s32[]{:T(128)}) while((s32[]{:T(128)}, f32[8,272,272]{2,1,0:T(8,128)}, s32[7,3]{0,1:T(4,128)S(1)}, f32[7,8,16,16]{3,2,1,0:T(8,128)S(1)}, s32[]{:T(128)}, ...), condition=%wide.region_5.6_spmd, body=%wide.region_4.5_spmd.sunk | while | flops 2056 | bytes 41141 | solution.py:133
  649.0 4.3 dynamic_update_slice.8
  659.0 4.3 dynamic_update_slice.8
  668.9 4.2 dynamic_update_slice.8
  678.8 4.3 dynamic_update_slice.8
  688.8 4.3 dynamic_update_slice.8
  698.8 4.3 dynamic_update_slice.8
  708.8 4.3 dynamic_update_slice.8
  719.0 33.1 %reduce-scatter.2.cloned.1.call-done = f32[8,32,256]{2,1,0:T(8,128)} async-done(((f32[8,256,256]{2,1,0:T(8,128)}), f32[8,32,256]{2,1,0:T(8,128)}) %reduce-scatter.2.cloned.1.call-update) | async-done | bytes 262160 | tf_op jit(solution)/shard_map/reduce_scatter | solution.py:137
  (92 shorter events, 47.2 us)
Async XLA Ops:
  7.2 105.8 %copy-start = (f32[128,16,256]{2,1,0:T(8,128)S(1)}, f32[128,16,256]{2,1,0:T(8,128)}, u32[]{:S(2)}) copy-start(f32[128,16,256]{2,1,0:T(8,128)} %param.12) | copy-start | bytes 6291460
  7.2 6.8 copy-start.6
  15.4 14.9 %copy-start.11 = (s32[64,3]{0,1:T(4,128)S(1)}, s32[64,3]{0,1:T(4,128)}, u32[]{:S(2)}) copy-start(s32[64,3]{0,1:T(4,128)} %param.13) | copy-start | bytes 2308
  15.4 15.0 %copy-start.9 = (s32[1,7]{1,0:T(1,128)S(1)}, s32[1,7]{1,0:T(1,128)}, u32[]{:S(2)}) copy-start(s32[1,7]{1,0:T(1,128)} %param.14) | copy-start | bytes 88
  18.4 12.8 %copy-start.8 = (s32[22016]{0:T(1024)S(1)}, s32[22016]{0:T(1024)}, u32[]{:S(2)}) copy-start(s32[22016]{0:T(1024)} %param.10) | copy-start | bytes 264196
  18.4 99.8 %all-to-all-start = ((f32[2,1,256,688]{3,1,0,2:T(1,128)}), f32[2,1,256,688]{3,1,0,2:T(1,128)}, u32[]{:S(2)}, u32[]{:S(2)}) async-start(f32[2,1,256,688]{3,1,0,2:T(1,128)} %copy.61), calls=%async_computation | async-start | bytes 3145728 | tf_op jit(solution)/shard_map/all_to_all | solution.py:93
  30.3 520.9 %all-reduce.8.cloned.1.call-start = ((), (), s32[]{:S(2)}) async-start(), calls=%async_computation.5 | async-start | bytes 262144
  298.9 4.6 copy-start.5
  307.3 2.4 copy-start.1
  309.7 1.3 copy-start.3
  396.8 9.8 %copy-start.10 = (s32[128]{0:T(128)S(1)}, s32[128]{0:T(128)}, u32[]{:S(2)}) copy-start(s32[128]{0:T(128)} %param.15) | copy-start | bytes 1540
  396.8 11.4 %copy-start.12 = (u32[256]{0:T(256)S(1)}, u32[256]{0:T(256)}, u32[]{:S(2)}) copy-start(u32[256]{0:T(256)} %constant.145) | copy-start | bytes 3076
  407.6 210.2 %all-reduce.6.cloned.1.call-start = ((), (), s32[]{:S(2)}) async-start(), calls=%async_computation.3 | async-start | bytes 524288 | tf_op jit(solution)/shard_map/psum | solution.py:109
  620.5 19.9 %all-to-all-start.1 = ((f32[32,4,512]{2,1,0:T(4,128)}), f32[32,4,512]{2,1,0:T(4,128)S(1)}, u32[]{:S(2)}, u32[]{:S(2)}) async-start(f32[32,4,512]{2,1,0:T(4,128)} %stack.20), calls=%async_computation.1 | async-start | bytes 524288 | tf_op jit(solution)/shard_map/all_to_all | solution.py:12
  630.7 121.5 %reduce-scatter.2.cloned.1.call-start = ((), (), s32[]{:S(2)}) async-start(), calls=%async_computation.4 | async-start | bytes 2359296 | tf_op jit(solution)/shard_map/reduce_scatter | solution.py:137
  714.1 2.5 copy-start.2
  714.1 3.2 copy-start.4
  717.2 34.9 %copy-start.7 = (f32[4,128,128]{2,1,0:T(8,128)S(1)}, f32[4,128,128]{2,1,0:T(8,128)}, u32[]{:S(2)}) copy-start(f32[4,128,128]{2,1,0:T(8,128)} %all-reduce.6.cloned.1.call-done) | copy-start | bytes 786436
Sparse Core Ops, SparseCore 0:
  407.7 143.4 all-reduce.7
  554.1 63.6 all-reduce.5
  719.2 32.9 reduce-scatter.1
